TPU v7x, 128 devices: a whole 4x4x4 slice. The times are simulated.
128 devices in a mesh: pipe: 16 (over y_lo, z, core), seq: 8 (over x, y_hi).
Axes of the slice: x: 4, y: 4 (y_hi: 2, y_lo: 2; y = y_hi * 2 + y_lo), z: 4, core: 2. Of those that a mesh axis runs over, the one named last changes fastest.
Arguments:
- x_fwd: float32 [16, 1024, 2048], P('pipe', 'seq'), may hold values from -12 to 12
- x_bwd: float32 [16, 1024, 2048], P('pipe', 'seq'), may hold values from -12 to 12
- grad_in: float32 [16, 1024, 2048], P('pipe', 'seq'), may hold values from -6 to 6
- gain: float32 [16, 2048], P('pipe'), may hold values from 0.25 to 1.75
- w_query: bfloat16 [16, 2048, 2048], P('pipe', None, 'seq'), may hold values from -2 to 2
- w_key: bfloat16 [16, 2048, 2048], P('pipe', None, 'seq'), may hold values from -2 to 2
- w_value: bfloat16 [16, 2048, 2048], P('pipe', None, 'seq'), may hold values from -0.125 to 0.125
- w_out: bfloat16 [16, 2048, 2048], P('pipe', None, 'seq'), may hold values from -0.125 to 0.125
Outputs:
- act_next: float32 [16, 1024, 2048], P('pipe', 'seq')
- grad_prev: float32 [16, 1024, 2048], P('pipe', 'seq')
All inputs are finite; a program needn't handle non-finite values.
Results may differ from a plain program's by a relative error of at most 0.012.
The roundings to bfloat16 on the way count: a program that leaves them out, or rounds other values in their place, can miss the bound.
Values may be sent and summed in bfloat16 or wider, within the bound.
A program may use at most 192 MiB of HBM per device.

v0:
```python
import jax
import jax.numpy as jnp
from jax import lax
from jax.sharding import PartitionSpec as P

HD = 128


def passed_along(value, axis, steps):
    count = lax.axis_size(axis)
    pairs = [(source, (source + steps) % count) for source in range(count)]
    return lax.ppermute(value, axis, pairs)


def rope_tables(positions):
    half_dim = HD // 2
    inverse = 10000.0 ** (-(jnp.arange(half_dim).astype(jnp.float32) * 2.0 / HD))
    angles = positions.astype(jnp.float32)[:, None] * inverse[None, :]
    return (jnp.cos(angles)[:, None, :], jnp.sin(angles)[:, None, :])


def rotate(values, cosine, sine_table):
    shaped = values.reshape(values.shape[0], -1, HD)
    first_half = shaped[..., : HD // 2]
    second_half = shaped[..., HD // 2 :]
    output = jnp.concatenate(
        [
            first_half * cosine - second_half * sine_table,
            second_half * cosine + first_half * sine_table,
        ],
        -1,
    )
    return output.reshape(values.shape)


def rotate_back(values, cosine, sine_table):
    shaped = values.reshape(values.shape[0], -1, HD)
    first_half = shaped[..., : HD // 2]
    second_half = shaped[..., HD // 2 :]
    output = jnp.concatenate(
        [
            first_half * cosine + second_half * sine_table,
            second_half * cosine - first_half * sine_table,
        ],
        -1,
    )
    return output.reshape(values.shape)


def normalize(inputs, gain_row):
    inv_rms = lax.rsqrt(jnp.mean(inputs * inputs, -1, keepdims=True) + 1e-05)
    return ((inputs * inv_rms * gain_row).astype(jnp.bfloat16), inv_rms)


def times_t(left, right):
    return lax.dot_general(
        left, right, (((1,), (1,)), ((), ())), preferred_element_type=jnp.float32
    )


def split_heads(values):
    return values.reshape(values.shape[0], -1, HD)


def attend(query, key_rows, value_rows):
    length = query.shape[0]
    score_scale = HD ** (-0.5)
    key_heads = split_heads(key_rows)
    value_heads = split_heads(value_rows)
    query_blocks = split_heads(query).reshape(length // length, length, -1, HD)

    def one_block(query_block):
        scores = (
            jnp.einsum("qhd,khd->hqk", query_block, key_heads, preferred_element_type=jnp.float32)
            * score_scale
        )
        probs = jax.nn.softmax(scores, axis=-1)
        output = jnp.einsum(
            "hqk,khd->qhd",
            probs.astype(jnp.bfloat16),
            value_heads,
            preferred_element_type=jnp.float32,
        )
        return output.astype(jnp.bfloat16)

    return lax.map(one_block, query_blocks).reshape(length, -1)


def attend_back(query, key_rows, value_rows, grad_out, cosine, sine_table):
    length = query.shape[0]
    score_scale = HD ** (-0.5)
    key_heads = split_heads(key_rows)
    value_heads = split_heads(value_rows)
    query_blocks = split_heads(query).reshape(length // length, length, -1, HD)
    grad_blocks = split_heads(grad_out).reshape(length // length, length, -1, HD)

    def step(totals, operands):
        query_block, grad_block = operands
        scores = (
            jnp.einsum("qhd,khd->hqk", query_block, key_heads, preferred_element_type=jnp.float32)
            * score_scale
        )
        probs = jax.nn.softmax(scores, axis=-1)
        value_grad = jnp.einsum(
            "hqk,qhd->khd",
            probs.astype(jnp.bfloat16),
            grad_block,
            preferred_element_type=jnp.float32,
        )
        prob_grad = jnp.einsum(
            "qhd,khd->hqk", grad_block, value_heads, preferred_element_type=jnp.float32
        )
        row_delta = jnp.sum(probs * prob_grad, -1, keepdims=True)
        score_grad = (probs * (prob_grad - row_delta) * score_scale).astype(jnp.bfloat16)
        query_grad = jnp.einsum(
            "hqk,khd->qhd", score_grad, key_heads, preferred_element_type=jnp.float32
        )
        key_grad = jnp.einsum(
            "hqk,qhd->khd", score_grad, query_block, preferred_element_type=jnp.float32
        )
        return ((totals[0] + key_grad, totals[1] + value_grad), query_grad)

    zero_heads = jnp.zeros(key_heads.shape, jnp.float32)
    (key_total, value_total), query_grads = lax.scan(
        step, (zero_heads, zero_heads), (query_blocks, grad_blocks)
    )
    query_grad = rotate_back(query_grads.reshape(length, -1), cosine, sine_table).astype(
        jnp.bfloat16
    )
    key_grad = rotate_back(key_total.reshape(length, -1), cosine, sine_table).astype(jnp.bfloat16)
    return (query_grad, key_grad, value_total.reshape(length, -1).astype(jnp.bfloat16))


def shards(x_fwd, x_bwd, grad_in, gain, w_query, w_key, w_value, w_out):
    act_in = x_fwd[0]
    saved_in = x_bwd[0]
    grad = grad_in[0]
    gain_row = gain[0]
    local_rows = act_in.shape[0]
    length = local_rows * lax.axis_size("seq")
    normed_fwd, inv_fwd = normalize(act_in, gain_row)
    normed_bwd, inv_bwd = normalize(saved_in, gain_row)
    grad_low = grad.astype(jnp.bfloat16)
    full_cos, full_sin = rope_tables(jnp.arange(length))
    all_fwd = lax.all_gather(normed_fwd, "seq", axis=0, tiled=True)
    all_bwd = lax.all_gather(normed_bwd, "seq", axis=0, tiled=True)
    all_grad = lax.all_gather(grad_low, "seq", axis=0, tiled=True)

    def project(normed):
        query = rotate(
            jnp.dot(normed, w_query[0], preferred_element_type=jnp.float32), full_cos, full_sin
        ).astype(jnp.bfloat16)
        key_rows = rotate(
            jnp.dot(normed, w_key[0], preferred_element_type=jnp.float32), full_cos, full_sin
        ).astype(jnp.bfloat16)
        value_rows = jnp.dot(normed, w_value[0], preferred_element_type=jnp.float32).astype(
            jnp.bfloat16
        )
        return (query, key_rows, value_rows)

    attn = attend(*project(all_fwd))
    branch = lax.psum_scatter(
        times_t(attn, w_out[0]).astype(jnp.bfloat16), "seq", scatter_dimension=0, tiled=True
    )
    attn_grad = jnp.dot(all_grad, w_out[0], preferred_element_type=jnp.float32).astype(jnp.bfloat16)
    query_b, key_b, value_b = project(all_bwd)
    query_grad, key_grad, value_grad = attend_back(
        query_b, key_b, value_b, attn_grad, full_cos, full_sin
    )
    d_normed = lax.psum_scatter(
        (
            times_t(query_grad, w_query[0])
            + times_t(key_grad, w_key[0])
            + times_t(value_grad, w_value[0])
        ).astype(jnp.bfloat16),
        "seq",
        scatter_dimension=0,
        tiled=True,
    ).astype(jnp.float32)
    act_out = act_in + branch.astype(jnp.float32)
    gain_grad = d_normed * gain_row
    d_input = inv_bwd * gain_grad - saved_in * inv_bwd * inv_bwd * inv_bwd * jnp.mean(
        saved_in * gain_grad, -1, keepdims=True
    )
    sent_forward = passed_along(act_out.astype(jnp.bfloat16), "pipe", 1).astype(act_out.dtype)
    sent_backward = passed_along((grad + d_input).astype(jnp.bfloat16), "pipe", -1).astype(
        jnp.float32
    )
    return (sent_forward[None], sent_backward[None])


def solution(mesh):
    placed = (
        P("pipe", "seq", None),
        P("pipe", "seq", None),
        P("pipe", "seq", None),
        P("pipe", None),
        P("pipe", None, "seq"),
        P("pipe", None, "seq"),
        P("pipe", None, "seq"),
        P("pipe", None, "seq"),
    )
    return jax.shard_map(
        shards,
        mesh=mesh,
        in_specs=placed,
        out_specs=(P("pipe", "seq", None), P("pipe", "seq", None)),
        check_vma=False,
    )
```

profile of v0, /device:TPU:0, one launch (start us, length us, event | category | flops | bytes accessed | tf_op | source)
XLA Modules:
  0.0 437.1 jit_solution(6163161213774346154)
XLA Ops:
  10.2 2.8 multiply_convert_fusion.1
  13.0 2.1 bitcast_convert_fusion
  20.6 66.6 %all-gather.6.cloned.1.call-done = bf16[1024,2048]{1,0:T(8,128)(2,1)} async-done(((bf16[128,2048]{1,0:T(8,128)(2,1)}), bf16[1024,2048]{1,0:T(8,128)(2,1)}) %all-gather.6.cloned.1.call-update) | async-done | bytes 4194320 | tf_op jit(solution)/shard_map/all_gather | solution.py:146
  87.2 3.8 fusion.14
  91.0 3.8 fusion.12
  96.2 7.3 %fusion.79 = (f32[2,1024]{1,0:T(2,128)S(1)}, f32[2,1024,1024]{1,2,0:T(8,128)}) fusion(bf16[1024,2,64]{0,2,1:T(8,128)(2,1)} %get-tuple-element.38, bf16[1024,2,64]{0,2,1:T(8,128)(2,1)} %get-tuple-element.37, bf16[1024,2,64]{0,2,1:T(8,128)(2,1)} %get-tuple-element.59, bf16[1024,2,64]{0,2,1:T(8,128)(2,1)} %get-tuple-element.60), kind=kOutput, calls=%fused_computation.107 | convolution fusion | flops 545260544 | bytes 9445376 | tf_op jit(solution)/shard_map/while/body/eval_jaxpr/sub | solution.py:103
  103.4 4.3 convolution_convert_fusion.1
  107.7 51.2 %all-gather.8.cloned.1.call-done = bf16[1024,2048]{1,0:T(8,128)(2,1)} async-done(((bf16[128,2048]{1,0:T(8,128)(2,1)}), bf16[1024,2048]{1,0:T(8,128)(2,1)}) %all-gather.8.cloned.1.call-update) | async-done | bytes 4194320 | tf_op jit(solution)/shard_map/all_gather | solution.py:147
  159.0 3.8 convolution_convert_fusion.2
  163.6 4.5 %fusion.81 = f32[2,1024,1024]{1,2,0:T(8,128)} fusion(bf16[1024,2,128]{0,2,1:T(8,128)(2,1)S(1)} %bitcast.110, bf16[1024,2,128]{0,2,1:T(8,128)(2,1)S(1)} %bitcast.112), kind=kOutput, calls=%fused_computation.109 | convolution fusion | flops 536870912 | bytes 9437184 | tf_op jit(solution)/shard_map/while/body/eval_jaxpr/qhd,khd->hqk/dot_general | solution.py:110
  168.2 15.4 %fusion.34 = f32[1024,2,128]{0,2,1:T(8,128)} fusion(f32[2,1024,1024]{1,2,0:T(8,128)} %fusion.81, bf16[1024,2,64]{0,2,1:T(8,128)(2,1)} %get-tuple-element.38, bf16[1024,2,64]{0,2,1:T(8,128)(2,1)} %get-tuple-element.37, f32[2,1024,1024]{1,2,0:T(8,128)} %get-tuple-element.66, f32[2,1024]{1,0:T(2,128)S(1)} %get-tuple-element.65), kind=kOutput, calls=%fused_computation.32 | convolution fusion | flops 552602624 | bytes 18358272 | tf_op jit(solution)/shard_map/while/body/eval_jaxpr/hqk,qhd->khd/dot_general | solution.py:118
  183.6 14.9 %fusion.31 = f32[1024,2,128]{0,2,1:T(8,128)} fusion(f32[2,1024,1024]{1,2,0:T(8,128)} %fusion.81, bf16[1024,2,64]{0,2,1:T(8,128)(2,1)} %get-tuple-element.59, bf16[1024,2,64]{0,2,1:T(8,128)(2,1)} %get-tuple-element.60, f32[2,1024,1024]{1,2,0:T(8,128)} %get-tuple-element.66, f32[2,1024]{1,0:T(2,128)S(1)} %get-tuple-element.65), kind=kOutput, calls=%fused_computation.31 | convolution fusion | flops 552602624 | bytes 18358272 | tf_op jit(solution)/shard_map/while/body/eval_jaxpr/hqk,khd->qhd/dot_general | solution.py:115
  198.5 5.9 %fusion.38 = bf16[2,128,1024]{2,1,0:T(8,128)(2,1)} fusion(bf16[1024,2,128]{0,2,1:T(8,128)(2,1)} %bitcast.111, f32[2,1024,1024]{1,2,0:T(8,128)} %get-tuple-element.66, f32[2,1024]{1,0:T(2,128)S(1)} %get-tuple-element.65), kind=kOutput, calls=%fused_computation.34 | convolution fusion | flops 541327360 | bytes 9445376 | tf_op jit(solution)/shard_map/while/body/eval_jaxpr/hqk,qhd->khd/dot_general | solution.py:104
  204.4 26.3 %all-gather.4.cloned.1.call-done = bf16[1024,2048]{1,0:T(8,128)(2,1)} async-done(((bf16[128,2048]{1,0:T(8,128)(2,1)}), bf16[1024,2048]{1,0:T(8,128)(2,1)}) %all-gather.4.cloned.1.call-update) | async-done | bytes 4194320 | tf_op jit(solution)/shard_map/all_gather | solution.py:145
  230.7 3.9 fusion.16
  234.6 3.8 fusion.18
  243.0 3.4 add_convert_fusion
  246.5 5.2 %fusion.80 = (f32[2,1024]{1,0:T(2,128)S(1)}, f32[2,1024,1024]{1,2,0:T(8,128)}) fusion(bf16[1024,2,64]{0,2,1:T(8,128)(2,1)S(1)} %copy-done.13, bf16[1024,2,64]{0,2,1:T(8,128)(2,1)S(1)} %copy-done.14, bf16[1024,2,64]{0,2,1:T(8,128)(2,1)S(1)} %copy-done.15, bf16[1024,2,64]{0,2,1:T(8,128)(2,1)S(1)} %copy-done.16), kind=kOutput, calls=%fused_computation.108 | convolution fusion | flops 545260544 | bytes 9445376 | tf_op jit(solution)/shard_map/while/body/eval_jaxpr/sub | solution.py:77
  251.7 3.8 convolution_convert_fusion.3
  257.9 3.3 convolution_convert_fusion
  261.2 68.6 %reduce-scatter.5.cloned.1.call-done = bf16[128,2048]{1,0:T(8,128)(2,1)} async-done(((bf16[1024,2048]{1,0:T(8,128)(2,1)}), bf16[128,2048]{1,0:T(8,128)(2,1)}) %reduce-scatter.5.cloned.1.call-update) | async-done | bytes 524304 | tf_op jit(solution)/shard_map/reduce_scatter | solution.py:170
  331.0 2.5 fusion.43
  334.4 83.1 %reduce-scatter.3.cloned.1.call-done = bf16[128,2048]{1,0:T(8,128)(2,1)} async-done(((bf16[1024,2048]{1,0:T(8,128)(2,1)}), bf16[128,2048]{1,0:T(8,128)(2,1)}) %reduce-scatter.3.cloned.1.call-update) | async-done | bytes 524304 | tf_op jit(solution)/shard_map/reduce_scatter | solution.py:162
  419.9 9.6 %collective-permute-done = bf16[128,2048]{1,0:T(8,128)(2,1)S(1)} collective-permute-done((bf16[128,2048]{1,0:T(8,128)(2,1)S(1)}, bf16[128,2048]{1,0:T(8,128)(2,1)S(1)}, u32[]{:S(2)}, u32[]{:S(2)}) %collective-permute-start) | collective-permute-done | bytes 524320 | tf_op jit(solution)/shard_map/ppermute | solution.py:12
  (71 shorter events, 23.2 us)
Async XLA Ops:
  7.2 96.3 %copy-start = (bf16[1,2048,256]{2,1,0:T(8,128)(2,1)S(1)}, bf16[1,2048,256]{2,1,0:T(8,128)(2,1)}, u32[]{:S(2)}) copy-start(bf16[1,2048,256]{2,1,0:T(8,128)(2,1)} %param.14) | copy-start | bytes 3145732
  7.2 8.8 %copy-start.4 = (bf16[1,2048,256]{2,1,0:T(8,128)(2,1)S(1)}, bf16[1,2048,256]{2,1,0:T(8,128)(2,1)}, u32[]{:S(2)}) copy-start(bf16[1,2048,256]{2,1,0:T(8,128)(2,1)} %param.13) | copy-start | bytes 3145732
  7.2 10.2 %copy-start.3 = (bf16[1,2048,256]{2,1,0:T(8,128)(2,1)S(1)}, bf16[1,2048,256]{2,1,0:T(8,128)(2,1)}, u32[]{:S(2)}) copy-start(bf16[1,2048,256]{2,1,0:T(8,128)(2,1)} %param.12) | copy-start | bytes 3145732
  7.2 80.0 %all-gather.6.cloned.1.call-start = ((), (), s32[]{:S(2)}) async-start(), calls=%async_computation.4 | async-start | bytes 4718592 | tf_op jit(solution)/shard_map/all_gather | solution.py:146
  13.0 146.0 %all-gather.8.cloned.1.call-start = ((), (), s32[]{:S(2)}) async-start(), calls=%async_computation.5 | async-start | bytes 4718592 | tf_op jit(solution)/shard_map/all_gather | solution.py:147
  15.1 215.6 %all-gather.4.cloned.1.call-start = ((), (), s32[]{:S(2)}) async-start(), calls=%async_computation.2 | async-start | bytes 4718592 | tf_op jit(solution)/shard_map/all_gather | solution.py:145
  15.9 313.9 %reduce-scatter.5.cloned.1.call-start = ((), (), s32[]{:S(2)}) async-start(), calls=%async_computation.6 | async-start | bytes 4718592 | tf_op jit(solution)/shard_map/reduce_scatter | solution.py:170
  87.2 7.6 %copy-start.5 = (f32[1024,64]{0,1:T(8,128)S(1)}, f32[1024,64]{0,1:T(8,128)}, u32[]{:S(2)}) copy-start(f32[1024,64]{0,1:T(8,128)} %get-tuple-element.64) | copy-start | bytes 786436
  159.0 4.6 %copy-start.12 = (bf16[1024,256]{0,1:T(8,128)(2,1)S(1)}, bf16[1024,256]{0,1:T(8,128)(2,1)}, u32[]{:S(2)}) copy-start(bf16[1024,256]{0,1:T(8,128)(2,1)} %convolution_convert_fusion.1) | copy-start | bytes 1572868
  230.7 7.7 %copy-start.6 = (f32[1024,64]{0,1:T(8,128)S(1)}, f32[1024,64]{0,1:T(8,128)}, u32[]{:S(2)}) copy-start(f32[1024,64]{0,1:T(8,128)} %get-tuple-element.64) | copy-start | bytes 786436
  230.7 7.7 %copy-start.8 = (f32[1024,2,128]{0,2,1:T(8,128)S(1)}, f32[1024,2,128]{0,2,1:T(8,128)}, u32[]{:S(2)}) copy-start(f32[1024,2,128]{0,2,1:T(8,128)} %fusion.34) | copy-start | bytes 3145732
  230.7 7.7 %copy-start.9 = (f32[1024,2,128]{0,2,1:T(8,128)S(1)}, f32[1024,2,128]{0,2,1:T(8,128)}, u32[]{:S(2)}) copy-start(f32[1024,2,128]{0,2,1:T(8,128)} %fusion.31) | copy-start | bytes 3145732
  241.5 1.4 copy-start.10
  242.9 3.5 copy-start.13
  242.9 3.5 copy-start.14
  242.9 3.5 copy-start.15
  243.0 3.5 copy-start.16
  246.4 171.2 %reduce-scatter.3.cloned.1.call-start = ((), (), s32[]{:S(2)}) async-start(), calls=%async_computation.3 | async-start | bytes 4718592 | tf_op jit(solution)/shard_map/reduce_scatter | solution.py:162
  251.7 5.0 %copy-start.18 = (f32[2,1024,1024]{1,2,0:T(8,128)S(1)}, f32[2,1024,1024]{1,2,0:T(8,128)}, u32[]{:S(2)}) copy-start(f32[2,1024,1024]{1,2,0:T(8,128)} %get-tuple-element.68) | copy-start | bytes 25165828
  257.4 72.3 %copy-start.1 = (f32[1,128,2048]{2,1,0:T(8,128)S(1)}, f32[1,128,2048]{2,1,0:T(8,128)}, u32[]{:S(2)}) copy-start(f32[1,128,2048]{2,1,0:T(8,128)} %param.9) | copy-start | bytes 3145732
  257.4 72.3 %copy-start.17 = (f32[1,2048]{1,0:T(1,128)S(1)}, f32[1,2048]{1,0:T(1,128)}, u32[]{:S(2)}) copy-start(f32[1,2048]{1,0:T(1,128)} %param.11) | copy-start | bytes 24580
  257.9 159.7 %copy-start.2 = (f32[1,128,2048]{2,1,0:T(8,128)S(1)}, f32[1,128,2048]{2,1,0:T(8,128)}, u32[]{:S(2)}) copy-start(f32[1,128,2048]{2,1,0:T(8,128)} %param.8) | copy-start | bytes 3145732
  333.6 85.3 %collective-permute-start.1 = (bf16[128,2048]{1,0:T(8,128)(2,1)}, bf16[128,2048]{1,0:T(8,128)(2,1)S(1)}, u32[]{:S(2)}, u32[]{:S(2)}) collective-permute-start(bf16[128,2048]{1,0:T(8,128)(2,1)} %fusion.43), channel_id=1, source_target_pairs={{0,120},{8,0},{16,8},{24,16},{32,24},{40,32},{48,40},{56,48},{64,5... | collective-permute-start | bytes 1572872 | tf_op jit(solution)/shard_map/ppermute | solution.py:12
  418.7 10.8 %collective-permute-start = (bf16[128,2048]{1,0:T(8,128)(2,1)S(1)}, bf16[128,2048]{1,0:T(8,128)(2,1)S(1)}, u32[]{:S(2)}, u32[]{:S(2)}) collective-permute-start(bf16[128,2048]{1,0:T(8,128)(2,1)S(1)} %fusion.56), channel_id=1, source_target_pairs={{0,8},{8,16},{16,24},{24,32},{32,40},{40,48},{48,56},{56,64},{64,7... | collective-permute-start | bytes 1572872 | tf_op jit(solution)/shard_map/ppermute | solution.py:12
  (2 other events, 2.0 us)
Sparse Core Ops, SparseCore 0:
  13.1 74.0 all-gather.5
  89.5 69.4 all-gather.7
  161.3 69.3 all-gather.3
  246.5 83.1 reduce-scatter.4
  333.5 84.0 reduce-scatter.2
where the time goes:
time: 438 us; the launch traced here: 437 us
  waiting for transfers between devices  306 us (70%)
  matrix products  90.4 us (21%)
  other arithmetic  19.9 us (5%)
  between operations  14.1 us (3%)
  local copies, waits for them, and re-layouts  5.42 us (1%)
    reduce_scatter x1, waiting for transfers between devices, shards(): lax.psum_scatter(times_t(attn, w_out[0]).astype(jnp.bfloat16), 'seq', sca...  83.1 us
    reduce_scatter x1, waiting for transfers between devices, shards(): lax.psum_scatter((times_t(query_grad, w_query[0]) + times_t(key_grad, w_k...  68.6 us
    all_gather x1, waiting for transfers between devices, shards(): all_bwd = lax.all_gather(normed_bwd, 'seq', axis=0, tiled=True)  66.6 us
    all_gather x1, waiting for transfers between devices, shards(): all_grad = lax.all_gather(grad_low, 'seq', axis=0, tiled=True)  51.2 us
    all_gather x1, waiting for transfers between devices, shards(): all_fwd = lax.all_gather(normed_fwd, 'seq', axis=0, tiled=True)  26.3 us
    dot_general x1, matrix products, step(): jnp.einsum('hqk,qhd->khd', score_grad, query_block, preferred_element_typ...  15.4 us
    dot_general x1, matrix products, step(): jnp.einsum('hqk,khd->qhd', score_grad, key_heads, preferred_element_type=...  14.9 us
    ppermute x2, waiting for transfers between devices, passed_along(): return lax.ppermute(value, axis, pairs)  9.62 us
  transfers between devices with their start and end apart: 7, of which 6 were waited for; matrix products, arithmetic and copies ran while one was open for 21% of the time, Pallas kernels for 0%

commit v1 on v0

--- a/solution.py
+++ b/solution.py
@@ -143,7 +143,9 @@
     grad_low = grad.astype(jnp.bfloat16)
     full_cos, full_sin = rope_tables(jnp.arange(length))
     all_fwd = lax.all_gather(normed_fwd, "seq", axis=0, tiled=True)
-    all_bwd = lax.all_gather(normed_bwd, "seq", axis=0, tiled=True)
+    all_bwd = jnp.concatenate(
+        lax.all_to_all(jnp.stack([normed_bwd] * lax.axis_size("seq")), "seq", 0, 0), axis=0
+    )
     all_grad = lax.all_gather(grad_low, "seq", axis=0, tiled=True)
 
     def project(normed):

time: 438 us -> 392 us (0.89)
  waiting for transfers between devices: 306 us -> 252 us
  starting transfers between devices: 1.17 us -> 8.18 us
    all_gather x1 -> x0, waiting for transfers between devices: 66.6 us -> none  [shards(): all_bwd = lax.all_gather(normed_bwd, 'seq', axis=0, tiled=True)]
    all_to_all x0 -> x1, waiting for transfers between devices: none -> 63.6 us  [shards(): lax.all_to_all(jnp.stack([normed_bwd] * lax.axis_size('seq')), 'seq', 0, 0)]
    all_gather x1, waiting for transfers between devices: 51.2 us -> 0.93 us  [shards(): all_grad = lax.all_gather(grad_low, 'seq', axis=0, tiled=True)]
    all_to_all x0 -> x1, starting transfers between devices: none -> 7.04 us  [shards(): lax.all_to_all(jnp.stack([normed_bwd] * lax.axis_size('seq')), 'seq', 0, 0)]
  transfers between devices with their start and end apart: 7 -> 7, of which waited for: 6 -> 6; matrix products, arithmetic and copies ran while one was open for 21% -> 25% of each run, Pallas kernels for 0% -> 0%
where the time goes in v1:
time: 392 us
  waiting for transfers between devices  252 us (64%)
  matrix products  90.7 us (23%)
  other arithmetic  18.2 us (5%)
  between operations  14.1 us (4%)
  local copies, waits for them, and re-layouts  8.64 us (2%)
  starting transfers between devices  8.18 us (2%)
    reduce_scatter x1, waiting for transfers between devices, shards(): lax.psum_scatter(times_t(attn, w_out[0]).astype(jnp.bfloat16), 'seq', sca...  83.1 us
    reduce_scatter x1, waiting for transfers between devices, shards(): lax.psum_scatter((times_t(query_grad, w_query[0]) + times_t(key_grad, w_k...  68.5 us
    all_to_all x1, waiting for transfers between devices, shards(): lax.all_to_all(jnp.stack([normed_bwd] * lax.axis_size('seq')), 'seq', 0, 0)  63.6 us
    all_gather x1, waiting for transfers between devices, shards(): all_fwd = lax.all_gather(normed_fwd, 'seq', axis=0, tiled=True)  26.3 us
    dot_general x1, matrix products, step(): jnp.einsum('hqk,qhd->khd', score_grad, query_block, preferred_element_typ...  15.5 us
    dot_general x1, matrix products, step(): jnp.einsum('hqk,khd->qhd', score_grad, key_heads, preferred_element_type=...  15 us
    ppermute x2, waiting for transfers between devices, passed_along(): return lax.ppermute(value, axis, pairs)  9.62 us
    dot_general x4, matrix products, times_t(): lax.dot_general(left, right, (((1,), (1,)), ((), ())), preferred_element_...  9.26 us
  transfers between devices with their start and end apart: 7, of which 6 were waited for; matrix products, arithmetic and copies ran while one was open for 25% of the time, Pallas kernels for 0%

profile of v1, /device:TPU:0, one launch (start us, length us, event | category | flops | bytes accessed | tf_op | source)
XLA Modules:
  0.0 391.8 jit_solution(2905522748718804234)
XLA Ops:
  12.3 2.5 stack.5
  14.8 7.0 %all-to-all-start = ((bf16[8,128,2048]{2,1,0:T(8,128)(2,1)}), bf16[8,128,2048]{2,1,0:T(8,128)(2,1)}, u32[]{:S(2)}, u32[]{:S(2)}) async-start(bf16[8,128,2048]{2,1,0:T(8,128)(2,1)} %stack.5), calls=%async_computation.1 | async-start | bytes 8388608 | tf_op jit(solution)/shard_map/all_to_all | solution.py:147
  24.5 2.3 copy.34
  28.6 63.6 %all-to-all-done = bf16[8,128,2048]{2,1,0:T(8,128)(2,1)} async-done(((bf16[8,128,2048]{2,1,0:T(8,128)(2,1)}), bf16[8,128,2048]{2,1,0:T(8,128)(2,1)}, u32[]{:S(2)}, u32[]{:S(2)}) %all-to-all-start) | async-done | bytes 4194336 | tf_op jit(solution)/shard_map/all_to_all | solution.py:147
  92.2 3.8 fusion.84
  96.0 3.8 fusion.83
  101.2 7.2 %fusion.81 = (f32[2,1024]{1,0:T(2,128)S(1)}, f32[2,1024,1024]{1,2,0:T(8,128)}) fusion(bf16[1024,2,64]{0,2,1:T(8,128)(2,1)} %get-tuple-element.38, bf16[1024,2,64]{0,2,1:T(8,128)(2,1)} %get-tuple-element.37, bf16[1024,2,64]{0,2,1:T(8,128)(2,1)} %get-tuple-element.59, bf16[1024,2,64]{0,2,1:T(8,128)(2,1)} %get-tuple-element.60), kind=kOutput, calls=%fused_computation.108 | convolution fusion | flops 545260544 | bytes 9445376 | tf_op jit(solution)/shard_map/while/body/eval_jaxpr/sub | solution.py:103
  108.4 4.3 %convolution_convert_fusion.1 = bf16[1024,256]{0,1:T(8,128)(2,1)} fusion(bf16[1024,2048]{1,0:T(8,128)(2,1)} %bitcast.16, bf16[1,2048,256]{2,1,0:T(8,128)(2,1)S(1)} %copy-done), kind=kOutput, calls=%fused_computation.31 | convolution fusion | flops 1074003968 | bytes 5767168 | tf_op jit(solution)/shard_map/dot_general | solution.py:158
  113.6 3.8 convolution_convert_fusion.2
  118.3 4.5 %fusion.85 = f32[2,1024,1024]{1,2,0:T(8,128)} fusion(bf16[1024,2,128]{0,2,1:T(8,128)(2,1)S(1)} %bitcast.118, bf16[1024,2,128]{0,2,1:T(8,128)(2,1)S(1)} %bitcast.120), kind=kOutput, calls=%fused_computation.112 | convolution fusion | flops 536870912 | bytes 9437184 | tf_op jit(solution)/shard_map/while/body/eval_jaxpr/qhd,khd->hqk/dot_general | solution.py:110
  122.8 15.5 %fusion.30 = f32[1024,2,128]{0,2,1:T(8,128)} fusion(f32[2,1024,1024]{1,2,0:T(8,128)} %fusion.85, bf16[1024,2,64]{0,2,1:T(8,128)(2,1)} %get-tuple-element.38, bf16[1024,2,64]{0,2,1:T(8,128)(2,1)} %get-tuple-element.37, f32[2,1024,1024]{1,2,0:T(8,128)} %get-tuple-element.64, f32[2,1024]{1,0:T(2,128)S(1)} %get-tuple-element.63), kind=kOutput, calls=%fused_computation.28 | convolution fusion | flops 552602624 | bytes 18358272 | tf_op jit(solution)/shard_map/while/body/eval_jaxpr/hqk,qhd->khd/dot_general | solution.py:118
  138.3 15.0 %fusion.27 = f32[1024,2,128]{0,2,1:T(8,128)} fusion(f32[2,1024,1024]{1,2,0:T(8,128)} %fusion.85, bf16[1024,2,64]{0,2,1:T(8,128)(2,1)} %get-tuple-element.59, bf16[1024,2,64]{0,2,1:T(8,128)(2,1)} %get-tuple-element.60, f32[2,1024,1024]{1,2,0:T(8,128)} %get-tuple-element.64, f32[2,1024]{1,0:T(2,128)S(1)} %get-tuple-element.63), kind=kOutput, calls=%fused_computation.27 | convolution fusion | flops 552602624 | bytes 18358272 | tf_op jit(solution)/shard_map/while/body/eval_jaxpr/hqk,khd->qhd/dot_general | solution.py:115
  153.3 5.9 %fusion.34 = bf16[2,128,1024]{2,1,0:T(8,128)(2,1)} fusion(bf16[1024,2,128]{0,2,1:T(8,128)(2,1)} %bitcast.119, f32[2,1024,1024]{1,2,0:T(8,128)} %get-tuple-element.64, f32[2,1024]{1,0:T(2,128)S(1)} %get-tuple-element.63), kind=kOutput, calls=%fused_computation.30 | convolution fusion | flops 541327360 | bytes 9445376 | tf_op jit(solution)/shard_map/while/body/eval_jaxpr/hqk,qhd->khd/dot_general | solution.py:104
  159.2 26.3 %all-gather.3.cloned.1.call-done = bf16[1024,2048]{1,0:T(8,128)(2,1)} async-done(((bf16[128,2048]{1,0:T(8,128)(2,1)}), bf16[1024,2048]{1,0:T(8,128)(2,1)}) %all-gather.3.cloned.1.call-update) | async-done | bytes 4194320 | tf_op jit(solution)/shard_map/all_gather | solution.py:145
  185.5 3.9 fusion.12
  189.4 3.8 fusion.14
  197.7 3.4 add_convert_fusion
  201.2 5.2 %fusion.82 = (f32[2,1024]{1,0:T(2,128)S(1)}, f32[2,1024,1024]{1,2,0:T(8,128)}) fusion(bf16[1024,2,64]{0,2,1:T(8,128)(2,1)S(1)} %copy-done.13, bf16[1024,2,64]{0,2,1:T(8,128)(2,1)S(1)} %copy-done.14, bf16[1024,2,64]{0,2,1:T(8,128)(2,1)S(1)} %copy-done.15, bf16[1024,2,64]{0,2,1:T(8,128)(2,1)S(1)} %copy-done.16), kind=kOutput, calls=%fused_computation.109 | convolution fusion | flops 545260544 | bytes 9445376 | tf_op jit(solution)/shard_map/while/body/eval_jaxpr/sub | solution.py:77
  206.4 3.9 convolution_convert_fusion.3
  212.7 3.2 convolution_convert_fusion
  216.0 68.5 %reduce-scatter.5.cloned.1.call-done = bf16[128,2048]{1,0:T(8,128)(2,1)} async-done(((bf16[1024,2048]{1,0:T(8,128)(2,1)}), bf16[128,2048]{1,0:T(8,128)(2,1)}) %reduce-scatter.5.cloned.1.call-update) | async-done | bytes 524304 | tf_op jit(solution)/shard_map/reduce_scatter | solution.py:172
  285.7 2.5 fusion.43
  289.1 83.1 %reduce-scatter.3.cloned.1.call-done = bf16[128,2048]{1,0:T(8,128)(2,1)} async-done(((bf16[1024,2048]{1,0:T(8,128)(2,1)}), bf16[128,2048]{1,0:T(8,128)(2,1)}) %reduce-scatter.3.cloned.1.call-update) | async-done | bytes 524304 | tf_op jit(solution)/shard_map/reduce_scatter | solution.py:164
  374.6 9.6 %collective-permute-done = bf16[128,2048]{1,0:T(8,128)(2,1)S(1)} collective-permute-done((bf16[128,2048]{1,0:T(8,128)(2,1)S(1)}, bf16[128,2048]{1,0:T(8,128)(2,1)S(1)}, u32[]{:S(2)}, u32[]{:S(2)}) %collective-permute-start) | collective-permute-done | bytes 524320 | tf_op jit(solution)/shard_map/ppermute | solution.py:12
  (72 shorter events, 25.1 us)
Async XLA Ops:
  7.2 101.2 %copy-start = (bf16[1,2048,256]{2,1,0:T(8,128)(2,1)S(1)}, bf16[1,2048,256]{2,1,0:T(8,128)(2,1)}, u32[]{:S(2)}) copy-start(bf16[1,2048,256]{2,1,0:T(8,128)(2,1)} %param.14) | copy-start | bytes 3145732
  7.2 106.5 %all-gather.5.cloned.1.call-start = ((), (), s32[]{:S(2)}) async-start(), calls=%async_computation.5 | async-start | bytes 4718592 | tf_op jit(solution)/shard_map/all_gather | solution.py:149
  9.4 12.5 %copy-start.2 = (f32[1,128,2048]{2,1,0:T(8,128)S(1)}, f32[1,128,2048]{2,1,0:T(8,128)}, u32[]{:S(2)}) copy-start(f32[1,128,2048]{2,1,0:T(8,128)} %param.8) | copy-start | bytes 3145732
  9.4 12.6 %copy-start.17 = (f32[1,2048]{1,0:T(1,128)S(1)}, f32[1,2048]{1,0:T(1,128)}, u32[]{:S(2)}) copy-start(f32[1,2048]{1,0:T(1,128)} %param.11) | copy-start | bytes 24580
  12.3 10.8 %copy-start.3 = (bf16[1,2048,256]{2,1,0:T(8,128)(2,1)S(1)}, bf16[1,2048,256]{2,1,0:T(8,128)(2,1)}, u32[]{:S(2)}) copy-start(bf16[1,2048,256]{2,1,0:T(8,128)(2,1)} %param.13) | copy-start | bytes 3145732
  14.8 77.4 %all-to-all-start = ((bf16[8,128,2048]{2,1,0:T(8,128)(2,1)}), bf16[8,128,2048]{2,1,0:T(8,128)(2,1)}, u32[]{:S(2)}, u32[]{:S(2)}) async-start(bf16[8,128,2048]{2,1,0:T(8,128)(2,1)} %stack.5), calls=%async_computation.1 | async-start | bytes 8388608 | tf_op jit(solution)/shard_map/all_to_all | solution.py:147
  21.8 163.6 %all-gather.3.cloned.1.call-start = ((), (), s32[]{:S(2)}) async-start(), calls=%async_computation.3 | async-start | bytes 4718592 | tf_op jit(solution)/shard_map/all_gather | solution.py:145
  23.0 261.4 %reduce-scatter.5.cloned.1.call-start = ((), (), s32[]{:S(2)}) async-start(), calls=%async_computation.6 | async-start | bytes 4718592 | tf_op jit(solution)/shard_map/reduce_scatter | solution.py:172
  92.2 7.6 %copy-start.5 = (f32[1024,64]{0,1:T(8,128)S(1)}, f32[1024,64]{0,1:T(8,128)}, u32[]{:S(2)}) copy-start(f32[1024,64]{0,1:T(8,128)} %get-tuple-element.62) | copy-start | bytes 786436
  113.6 4.7 %copy-start.12 = (bf16[1024,256]{0,1:T(8,128)(2,1)S(1)}, bf16[1024,256]{0,1:T(8,128)(2,1)}, u32[]{:S(2)}) copy-start(bf16[1024,256]{0,1:T(8,128)(2,1)} %convolution_convert_fusion.1) | copy-start | bytes 1572868
  185.4 7.7 %copy-start.6 = (f32[1024,64]{0,1:T(8,128)S(1)}, f32[1024,64]{0,1:T(8,128)}, u32[]{:S(2)}) copy-start(f32[1024,64]{0,1:T(8,128)} %get-tuple-element.62) | copy-start | bytes 786436
  185.4 7.7 %copy-start.8 = (f32[1024,2,128]{0,2,1:T(8,128)S(1)}, f32[1024,2,128]{0,2,1:T(8,128)}, u32[]{:S(2)}) copy-start(f32[1024,2,128]{0,2,1:T(8,128)} %fusion.30) | copy-start | bytes 3145732
  185.5 7.7 %copy-start.9 = (f32[1024,2,128]{0,2,1:T(8,128)S(1)}, f32[1024,2,128]{0,2,1:T(8,128)}, u32[]{:S(2)}) copy-start(f32[1024,2,128]{0,2,1:T(8,128)} %fusion.27) | copy-start | bytes 3145732
  194.9 1.4 copy-start.4
  196.3 1.3 copy-start.10
  197.7 3.5 copy-start.13
  197.7 3.5 copy-start.14
  197.7 3.5 copy-start.15
  197.7 3.5 copy-start.16
  201.1 171.1 %reduce-scatter.3.cloned.1.call-start = ((), (), s32[]{:S(2)}) async-start(), calls=%async_computation.4 | async-start | bytes 4718592 | tf_op jit(solution)/shard_map/reduce_scatter | solution.py:164
  206.4 5.0 %copy-start.18 = (f32[2,1024,1024]{1,2,0:T(8,128)S(1)}, f32[2,1024,1024]{1,2,0:T(8,128)}, u32[]{:S(2)}) copy-start(f32[2,1024,1024]{1,2,0:T(8,128)} %get-tuple-element.66) | copy-start | bytes 25165828
  212.2 72.2 %copy-start.1 = (f32[1,128,2048]{2,1,0:T(8,128)S(1)}, f32[1,128,2048]{2,1,0:T(8,128)}, u32[]{:S(2)}) copy-start(f32[1,128,2048]{2,1,0:T(8,128)} %param.9) | copy-start | bytes 3145732
  288.2 85.3 %collective-permute-start.1 = (bf16[128,2048]{1,0:T(8,128)(2,1)}, bf16[128,2048]{1,0:T(8,128)(2,1)S(1)}, u32[]{:S(2)}, u32[]{:S(2)}) collective-permute-start(bf16[128,2048]{1,0:T(8,128)(2,1)} %fusion.43), channel_id=1, source_target_pairs={{0,120},{8,0},{16,8},{24,16},{32,24},{40,32},{48,40},{56,48},{64,5... | collective-permute-start | bytes 1572872 | tf_op jit(solution)/shard_map/ppermute | solution.py:12
  373.4 10.8 %collective-permute-start = (bf16[128,2048]{1,0:T(8,128)(2,1)S(1)}, bf16[128,2048]{1,0:T(8,128)(2,1)S(1)}, u32[]{:S(2)}, u32[]{:S(2)}) collective-permute-start(bf16[128,2048]{1,0:T(8,128)(2,1)S(1)} %fusion.57), channel_id=1, source_target_pairs={{0,8},{8,16},{16,24},{24,32},{32,40},{40,48},{48,56},{56,64},{64,7... | collective-permute-start | bytes 1572872 | tf_op jit(solution)/shard_map/ppermute | solution.py:12
  (2 other events, 2.0 us)
Sparse Core Ops, SparseCore 0:
  10.3 103.2 all-gather.4
  116.0 69.4 all-gather.2
  201.2 83.1 reduce-scatter.4
  288.2 84.0 reduce-scatter.2
